TPU v7x, 32 devices: a whole 2x2x4 slice. The times are simulated.
32 devices in a mesh: band: 2 (over x), grid: 16 (over z, y, core).
Axes of the slice: x: 2, y: 2, z: 4, core: 2. Of those that a mesh axis runs over, the one named last changes fastest.
Arguments:
- start_block: float32 [64, 128, 4, 128], P('band', 'grid'), may hold values from -6 to 6
- previous_block: float32 [64, 128, 4, 128], P('band', 'grid'), may hold values from -6 to 6
- previous_coupling: float32 [64, 64], replicated, may hold values from -0.75 to 0.75
- potential: float32 [128, 4, 128], P('grid'), may hold values from -2 to 2
- atom_cells: int32 [128, 128], P('grid'), may hold values from 0 to 7167, as said below
- atom_proj: float32 [128, 4, 128], P('grid'), may hold values from -1.08 to 1.08
- atom_strength: float32 [128, 4], P('grid'), may hold values from 0.5 to 4
- atom_count: int32 [16], P('grid'), may hold values from 1 to 8, as said below
Outputs:
- a_blocks: float32 [2, 64, 64], P(None, None, 'band')
- b_blocks: float32 [2, 64, 64], P(None, None, 'band')
- final_block: float32 [64, 128, 4, 128], P('band', 'grid')
Inputs may be any that keep to these rules, and one draw needn't show every extreme that they name: `atom_cells`: row a lists 128 distinct cells of atom a's sphere as row-major indices over (14) planes x 4 x 128, counted from the first plane of the slab that holds row a; indices of 4096 or more lie in the first 6 planes of the next slab; on the last slab every index is below 4096. `atom_count`: slots at or past a slab's count are not atoms.
All inputs are finite; a program needn't handle non-finite values.
Results may differ from a plain program's by a relative error of at most 0.0003.
Values sent between devices are 32-bit elements; how exact they have to be, the bound alone decides.
A program may use at most 64 MiB of HBM per device.

v0:
```python
import jax
import jax.numpy as jnp
from jax import lax
from jax.sharding import PartitionSpec as P

NB = 64
STEPS = 2
HIGHEST = lax.Precision.HIGHEST
STENCIL_WEIGHTS = (
    -5369.0 / 1800.0,
    12.0 / 7.0,
    -15.0 / 56.0,
    10.0 / 189.0,
    -1.0 / 112.0,
    2.0 / 1925.0,
    -1.0 / 16632.0,
)


def extended_2(block, sides, width):
    for axis, dim in sides:
        count = lax.axis_size(axis)
        forward = [(i, i + 1) for i in range(count - 1)]
        backward = [(target, source) for source, target in forward]
        low = lax.ppermute(
            lax.slice_in_dim(block, block.shape[dim] - width, None, axis=dim), axis, forward
        )
        high = lax.ppermute(lax.slice_in_dim(block, 0, width, axis=dim), axis, backward)
        block = jnp.concatenate([low, block, high], axis=dim)
    return block


def from_behind(block, axis, distance):
    devices = range(lax.axis_size(axis))
    route = [(i - distance, i) for i in devices if i - distance in devices]
    return lax.ppermute(block, axis, route)


def kinetic_local(haloed, planes):
    center = haloed[:, 6 : 6 + planes]
    width_y, width_z = (center.shape[2], center.shape[3])
    padded = jnp.pad(center, ((0, 0), (0, 0), (6, 6), (6, 6)))
    laplace = 3.0 * STENCIL_WEIGHTS[0] * center
    for k in range(1, 7):
        laplace = laplace + STENCIL_WEIGHTS[k] * (
            haloed[:, 6 + k : 6 + k + planes] + haloed[:, 6 - k : 6 - k + planes]
        )
        laplace = laplace + STENCIL_WEIGHTS[k] * (
            padded[:, :, 6 + k : 6 + k + width_y, 6 : 6 + width_z]
            + padded[:, :, 6 - k : 6 - k + width_y, 6 : 6 + width_z]
        )
        laplace = laplace + STENCIL_WEIGHTS[k] * (
            padded[:, :, 6 : 6 + width_y, 6 + k : 6 + k + width_z]
            + padded[:, :, 6 : 6 + width_y, 6 - k : 6 - k + width_z]
        )
    return -0.5 * laplace


def projector_terms(extended, atom_cells, atom_proj, atom_strength, live_count):
    states_dev = extended.shape[0]
    atom_slots, points = atom_cells.shape
    cell_list = atom_cells.reshape(-1)
    picked = jnp.take(extended, cell_list, axis=1).reshape(states_dev, atom_slots, points)
    coefficient = jnp.einsum("sap,ajp->saj", picked, atom_proj, precision=HIGHEST)
    live_mask = (jnp.arange(atom_slots, dtype=jnp.int32) < live_count).astype(jnp.float32)
    scaled = coefficient * (atom_strength * live_mask[:, None])[None]
    spread = jnp.einsum("saj,ajp->sap", scaled, atom_proj, precision=HIGHEST)
    return jnp.zeros_like(extended).at[:, cell_list].add(spread.reshape(states_dev, -1))


def factor_of(gram):
    factor = jnp.linalg.cholesky(gram)
    identity = jnp.eye(gram.shape[0], dtype=jnp.float32)
    inverse = jax.scipy.linalg.solve_triangular(factor, identity, lower=True)
    return (factor, inverse)


def shards(
    start_block,
    previous_block,
    previous_coupling,
    potential,
    atom_cells,
    atom_proj,
    atom_strength,
    atom_count,
):
    states_dev, planes, width_y, width_z = start_block.shape
    cell_total = planes * lax.axis_size("grid") * width_y * width_z
    offset = lax.axis_index("band") * states_dev
    live_count = atom_count[0]
    a_list = []
    b_list = []

    def to_cells(block):
        return lax.all_to_all(block, "band", split_axis=1, concat_axis=0, tiled=True)

    def to_states(block):
        return lax.all_to_all(block, "band", split_axis=0, concat_axis=1, tiled=True)

    def summed(matrix):
        return lax.psum(matrix, ("band", "grid"))

    start_cells = to_cells(start_block)
    cell_shape = start_cells.shape
    start_flat = start_cells.reshape(NB, -1)
    factor, inverse = factor_of(
        summed(jnp.dot(start_flat, start_flat.T, precision=HIGHEST) / cell_total)
    )
    current_cells = jnp.dot(inverse, start_flat, precision=HIGHEST)
    previous_cells = to_cells(previous_block).reshape(NB, -1)
    coupling = previous_coupling
    current_local = to_states(current_cells.reshape(cell_shape))
    for iteration in range(STEPS):
        haloed = extended_2(current_local, (("grid", 1),), 6)
        kinetic_part = kinetic_local(haloed, planes)
        extended = haloed[:, 6:].reshape(states_dev, -1)
        terms = projector_terms(extended, atom_cells, atom_proj, atom_strength, live_count)
        terms = terms.reshape(states_dev, planes + 6, width_y, width_z)
        received = from_behind(terms[:, planes:], "grid", 1)
        own_terms = terms[:, :planes].at[:, :6].add(received)
        applied = kinetic_part + potential[None] * current_local + own_terms
        applied_cells = to_cells(applied).reshape(NB, -1)
        correlation = summed(
            jnp.dot(current_cells, applied_cells.T, precision=HIGHEST) / cell_total
        )
        residual_block = (
            applied_cells
            - jnp.dot(correlation.T, current_cells, precision=HIGHEST)
            - jnp.dot(coupling, previous_cells, precision=HIGHEST)
        )
        factor, inverse = factor_of(
            summed(jnp.dot(residual_block, residual_block.T, precision=HIGHEST) / cell_total)
        )
        coupling = factor.T
        a_list.append(lax.dynamic_slice_in_dim(correlation, offset, states_dev, 1))
        b_list.append(lax.dynamic_slice_in_dim(coupling, offset, states_dev, 1))
        previous_cells = current_cells
        current_cells = jnp.dot(inverse, residual_block, precision=HIGHEST)
        current_local = to_states(current_cells.reshape(cell_shape))
    return (jnp.stack(a_list), jnp.stack(b_list), current_local)


def solution(mesh):
    in_specs = (
        P("band", "grid", None, None),
        P("band", "grid", None, None),
        P(),
        P("grid", None, None),
        P("grid", None),
        P("grid", None, None),
        P("grid", None),
        P("grid"),
    )
    out_specs = (P(None, None, "band"), P(None, None, "band"), P("band", "grid", None, None))
    return jax.shard_map(shards, mesh=mesh, in_specs=in_specs, out_specs=out_specs, check_vma=False)
```

profile of v0, /device:TPU:0, one launch (start us, length us, event | category | flops | bytes accessed | tf_op | source)
XLA Modules:
  0.0 424.2 jit_solution(2157985983389813124)
XLA Ops:
  0.6 1.9 copy.51
  2.6 4.3 %all-to-all-start = ((f32[32,8,4,128]{3,2,0,1:T(4,128)}), f32[32,8,4,128]{3,2,0,1:T(4,128)S(1)}, u32[]{:S(2)}, u32[]{:S(2)}) async-start(f32[32,8,4,128]{3,2,0,1:T(4,128)} %copy.51), calls=%async_computation | async-start | bytes 1048576 | tf_op jit(solution)/shard_map/all_to_all | solution.py:96
  7.6 8.1 %all-to-all-done = f32[32,8,4,128]{3,2,0,1:T(4,128)S(1)} async-done(((f32[32,8,4,128]{3,2,0,1:T(4,128)}), f32[32,8,4,128]{3,2,0,1:T(4,128)S(1)}, u32[]{:S(2)}, u32[]{:S(2)}) %all-to-all-start) | async-done | bytes 524320 | tf_op jit(solution)/shard_map/all_to_all | solution.py:96
  16.5 40.0 %psum.35 = f32[64,64]{0,1:T(8,128)S(1)} all-reduce(f32[64,64]{0,1:T(8,128)S(1)} %convolution_multiply_fusion.4), channel_id=1, replica_groups=mesh['band'=2,'grid'=16] {'band','grid'}, use_global_device_ids=true, to_apply=%region_0.0 | all-reduce | flops 4096 | bytes 32768 | tf_op jit(solution)/shard_map/psum | solution.py:102
  56.6 5.8 %cholesky.59 = f32[64,64]{1,0:T(8,128)S(1)} custom-call(f32[64,64]{1,0:T(8,128)S(1)} %fusion.140), custom_call_target="Cholesky" | custom-call | tf_op jit(solution)/shard_map/jit(cholesky)/cholesky | solution.py:72
  63.1 0.7 fusion.134
  63.8 4.9 %custom-call.7 = f32[1,64,64]{1,2,0:T(8,128)S(1)} custom-call(f32[1,64,64]{2,1,0:T(8,128)S(1)} %fusion.134), custom_call_target="InvertDiagBlocksLowerTriangular" | custom-call | tf_op jit(solution)/shard_map/jit(_solve_triangular)/triangular_solve | solution.py:74
  69.5 1.1 reshape.180
  70.7 3.5 all-to-all-start.1
  74.3 7.9 %all-to-all-done.1 = f32[64,4,4,128]{3,2,1,0:T(4,128)S(1)} async-done(((f32[64,4,4,128]{3,2,1,0:T(4,128)}), f32[64,4,4,128]{3,2,1,0:T(4,128)S(1)}, u32[]{:S(2)}, u32[]{:S(2)}) %all-to-all-start.1) | async-done | bytes 524320 | tf_op jit(solution)/shard_map/all_to_all | solution.py:99
  82.4 0.8 fusion.145
  83.2 1.3 collective-permute-start
  84.5 2.3 collective-permute-done
  86.8 0.8 copy-done.3
  87.6 2.4 copy.56
  90.1 4.8 %gather_fusion = f32[1024,32]{1,0:T(8,128)S(1)} fusion(f32[32,7168]{0,1:T(8,128)} %bitcast.150, s32[1024]{0:T(1024)S(1)} %fusion.141), kind=kCustom, calls=%fused_computation.clone | custom fusion | bytes 266240 | tf_op jit(solution)/shard_map/jit(_take)/gather | solution.py:63
  96.3 8.0 %scatter_custom_fusion = f32[32,7168]{0,1:T(8,128)} fusion(s32[1024]{0:T(1024)S(1)} %bitcast.165, f32[1024,32]{1,0:T(8,128)S(1)} %copy.60, f32[]{:T(128)} %constant.127.clone.1), kind=kCustom, calls=%fused_computation.60 | custom fusion | flops 32768 | bytes 917508 | tf_op jit(solution)/shard_map/scatter-add | solution.py:68
  104.3 3.4 fusion.143
  107.7 1.2 copy.92
  108.9 8.3 %collective-permute-start.2 = (f32[32,6,4,128]{3,0,2,1:T(8,128)}, f32[32,6,4,128]{3,0,2,1:T(8,128)}, u32[]{:S(2)}, u32[]{:S(2)}) collective-permute-start(f32[32,6,4,128]{3,0,2,1:T(8,128)} %copy.92), channel_id=1, source_target_pairs={{0,1},{1,2},{2,3},{3,4},{4,5},{5,6},{6,7},{7,8},{8,9},{9,10},{10,1... | collective-permute-start | bytes 1179656 | tf_op jit(solution)/shard_map/ppermute | solution.py:36
  117.2 2.0 collective-permute-start.1
  119.3 0.9 copy.66
  120.2 4.2 all-to-all-start.3
  124.4 1.7 slice.410
  126.1 2.6 copy.91
  128.7 1.4 copy.90
  130.1 1.9 add_dynamic-update-slice_fusion.1
  132.0 4.3 %fusion.51 = f32[32,8,4,128]{3,0,2,1:T(8,128)} fusion(f32[32,8,4,128]{3,0,2,1:T(8,128)} %add_dynamic-update-slice_fusion.1, f32[32,8,4,128]{3,0,2,1:T(8,128)S(1)} %bitcast.145, f32[32,6,4,128]{3,0,2,1:T(8,128)} %collective-permute-done.1, f32[32,6,4,128]{3,0,2,1:T(8,128)} %copy-done.3, f32[8,4,128]{2,1,0:T(4,128)S(1)} %copy-done.7), kind=kLoop, calls=%fused_computation.150 | loop fusion | flops 8388608 | bytes 2375680 | tf_op jit(solution)/shard_map/add | solution.py:122
  136.4 3.7 all-to-all-start.2
  140.1 1.1 copy.102
  141.4 7.5 %all-to-all-done.2 = f32[32,8,4,128]{3,0,2,1:T(8,128)S(1)} async-done(((f32[32,8,4,128]{3,0,2,1:T(8,128)}), f32[32,8,4,128]{3,0,2,1:T(8,128)S(1)}, u32[]{:S(2)}, u32[]{:S(2)}) %all-to-all-start.2) | async-done | bytes 524320 | tf_op jit(solution)/shard_map/all_to_all | solution.py:96
  150.0 38.9 %psum.36 = f32[64,64]{0,1:T(8,128)S(1)} all-reduce(f32[64,64]{0,1:T(8,128)S(1)} %convolution_multiply_fusion.3), channel_id=1, replica_groups=mesh['band'=2,'grid'=16] {'band','grid'}, use_global_device_ids=true, to_apply=%region_4.8 | all-reduce | flops 4096 | bytes 32768 | tf_op jit(solution)/shard_map/psum | solution.py:102
  190.7 39.4 %psum.37 = f32[64,64]{0,1:T(8,128)S(1)} all-reduce(f32[64,64]{0,1:T(8,128)S(1)} %convolution_multiply_fusion.2), channel_id=1, replica_groups=mesh['band'=2,'grid'=16] {'band','grid'}, use_global_device_ids=true, to_apply=%region_5.9 | all-reduce | flops 4096 | bytes 32768 | tf_op jit(solution)/shard_map/psum | solution.py:102
  230.2 5.8 %cholesky.70 = f32[64,64]{1,0:T(8,128)S(1)} custom-call(f32[64,64]{1,0:T(8,128)S(1)} %fusion.138), custom_call_target="Cholesky" | custom-call | tf_op jit(solution)/shard_map/jit(cholesky)/cholesky | solution.py:72
  236.7 0.7 select_bitcast_fusion.1
  237.4 4.9 %custom-call.8 = f32[1,64,64]{1,2,0:T(8,128)S(1)} custom-call(f32[1,64,64]{2,1,0:T(8,128)S(1)} %get-tuple-element.32), custom_call_target="InvertDiagBlocksLowerTriangular" | custom-call | tf_op jit(solution)/shard_map/jit(_solve_triangular)/triangular_solve | solution.py:74
  243.5 10.8 %all_to_all.114 = f32[64,4,4,128]{3,2,1,0:T(4,128)S(1)} all-to-all(f32[64,4,4,128]{3,2,1,0:T(4,128)S(1)} %reshape.189), channel_id=1, replica_groups=mesh['band'=2,'grid'=16] {'band'}, dimensions={0} | all-to-all | bytes 1048576 | tf_op jit(solution)/shard_map/all_to_all | solution.py:99
  254.4 0.8 fusion.144
  255.3 1.3 collective-permute-start.3
  256.6 2.3 collective-permute-done.3
  258.9 0.7 copy-done.4
  259.7 2.4 copy.71
  262.1 4.8 %gather_fusion.1 = f32[1024,32]{1,0:T(8,128)S(1)} fusion(f32[32,7168]{0,1:T(8,128)} %bitcast.149, s32[1024]{0:T(1024)S(1)} %fusion.141), kind=kCustom, calls=%fused_computation.1.clone | custom fusion | bytes 266240 | tf_op jit(solution)/shard_map/jit(_take)/gather | solution.py:63
  268.4 8.0 %scatter_custom_fusion.1 = f32[32,7168]{0,1:T(8,128)} fusion(s32[1024]{0:T(1024)S(1)} %bitcast.166, f32[1024,32]{1,0:T(8,128)S(1)} %copy.74, f32[]{:T(128)} %constant.127.clone.1), kind=kCustom, calls=%fused_computation.58 | custom fusion | flops 32768 | bytes 917508 | tf_op jit(solution)/shard_map/scatter-add | solution.py:68
  276.4 3.3 fusion.142
  279.7 1.2 copy.95
  280.9 8.4 %collective-permute-start.5 = (f32[32,6,4,128]{3,0,2,1:T(8,128)}, f32[32,6,4,128]{3,0,2,1:T(8,128)}, u32[]{:S(2)}, u32[]{:S(2)}) collective-permute-start(f32[32,6,4,128]{3,0,2,1:T(8,128)} %copy.95), channel_id=1, source_target_pairs={{0,1},{1,2},{2,3},{3,4},{4,5},{5,6},{6,7},{7,8},{8,9},{9,10},{10,1... | collective-permute-start | bytes 1179656 | tf_op jit(solution)/shard_map/ppermute | solution.py:36
  289.3 2.0 collective-permute-start.4
  291.4 1.7 slice.437
  293.1 2.6 copy.94
  295.7 1.4 copy.93
  297.1 2.0 add_dynamic-update-slice_fusion
  299.0 4.5 %fusion.16 = f32[32,8,4,128]{3,0,2,1:T(8,128)} fusion(f32[32,8,4,128]{3,0,2,1:T(8,128)} %add_dynamic-update-slice_fusion, f32[32,8,4,128]{3,0,2,1:T(8,128)S(1)} %bitcast.148, f32[32,6,4,128]{3,0,2,1:T(8,128)} %collective-permute-done.4, f32[32,6,4,128]{3,0,2,1:T(8,128)} %copy-done.4, f32[8,4,128]{2,1,0:T(4,128)S(1)} %copy-done.7), kind=kLoop, calls=%fused_computation.115 | loop fusion | flops 8388608 | bytes 2375680 | tf_op jit(solution)/shard_map/add | solution.py:122
  303.5 3.5 all-to-all-start.5
  307.1 8.5 %all-to-all-done.5 = f32[32,8,4,128]{3,0,2,1:T(8,128)S(1)} async-done(((f32[32,8,4,128]{3,0,2,1:T(8,128)}), f32[32,8,4,128]{3,0,2,1:T(8,128)S(1)}, u32[]{:S(2)}, u32[]{:S(2)}) %all-to-all-start.5) | async-done | bytes 524320 | tf_op jit(solution)/shard_map/all_to_all | solution.py:96
  316.7 39.2 %psum.38 = f32[64,64]{0,1:T(8,128)S(1)} all-reduce(f32[64,64]{0,1:T(8,128)S(1)} %convolution_multiply_fusion.1), channel_id=1, replica_groups=mesh['band'=2,'grid'=16] {'band','grid'}, use_global_device_ids=true, to_apply=%region_7.11 | all-reduce | flops 4096 | bytes 32768 | tf_op jit(solution)/shard_map/psum | solution.py:102
  357.8 40.5 %psum.39 = f32[64,64]{0,1:T(8,128)S(1)} all-reduce(f32[64,64]{0,1:T(8,128)S(1)} %convolution_multiply_fusion), channel_id=1, replica_groups=mesh['band'=2,'grid'=16] {'band','grid'}, use_global_device_ids=true, to_apply=%region_8.12 | all-reduce | flops 4096 | bytes 32768 | tf_op jit(solution)/shard_map/psum | solution.py:102
  398.3 5.8 %cholesky.81 = f32[64,64]{1,0:T(8,128)S(1)} custom-call(f32[64,64]{1,0:T(8,128)S(1)} %fusion.136), custom_call_target="Cholesky" | custom-call | tf_op jit(solution)/shard_map/jit(cholesky)/cholesky | solution.py:72
  404.8 0.7 select_bitcast_fusion
  405.5 4.9 %custom-call.9 = f32[1,64,64]{1,2,0:T(8,128)S(1)} custom-call(f32[1,64,64]{2,1,0:T(8,128)S(1)} %get-tuple-element.30), custom_call_target="InvertDiagBlocksLowerTriangular" | custom-call | tf_op jit(solution)/shard_map/jit(_solve_triangular)/triangular_solve | solution.py:74
  411.2 1.1 reshape.195
  412.4 3.5 all-to-all-start.6
  417.2 6.2 %all-to-all-done.6 = f32[64,4,4,128]{3,2,1,0:T(4,128)S(1)} async-done(((f32[64,4,4,128]{3,2,1,0:T(4,128)}), f32[64,4,4,128]{3,2,1,0:T(4,128)S(1)}, u32[]{:S(2)}, u32[]{:S(2)}) %all-to-all-start.6) | async-done | bytes 524320 | tf_op jit(solution)/shard_map/all_to_all | solution.py:99
  423.4 0.9 copy.82
  (84 shorter events, 16.5 us)
Async XLA Ops:
  0.6 188.9 %copy-start = (f32[64,64]{1,0:T(8,128)S(1)}, f32[64,64]{1,0:T(8,128)}, u32[]{:S(2)}) copy-start(f32[64,64]{1,0:T(8,128)} %param.19) | copy-start | bytes 49156
  2.6 71.6 %copy-start.9 = (f32[8,4]{0,1:T(4,128)S(1)}, f32[8,4]{0,1:T(4,128)}, u32[]{:S(2)}) copy-start(f32[8,4]{0,1:T(4,128)} %param.23) | copy-start | bytes 388
  2.6 71.7 %copy-start.8 = (s32[8,128]{1,0:T(8,128)S(1)}, s32[8,128]{1,0:T(8,128)}, u32[]{:S(2)}) copy-start(s32[8,128]{1,0:T(8,128)} %param.21) | copy-start | bytes 12292
  2.6 13.1 %all-to-all-start = ((f32[32,8,4,128]{3,2,0,1:T(4,128)}), f32[32,8,4,128]{3,2,0,1:T(4,128)S(1)}, u32[]{:S(2)}, u32[]{:S(2)}) async-start(f32[32,8,4,128]{3,2,0,1:T(4,128)} %copy.51), calls=%async_computation | async-start | bytes 1048576 | tf_op jit(solution)/shard_map/all_to_all | solution.py:96
  70.7 11.5 %all-to-all-start.1 = ((f32[64,4,4,128]{3,2,1,0:T(4,128)}), f32[64,4,4,128]{3,2,1,0:T(4,128)S(1)}, u32[]{:S(2)}, u32[]{:S(2)}) async-start(f32[64,4,4,128]{3,2,1,0:T(4,128)} %reshape.180), calls=%async_computation.1 | async-start | bytes 1048576 | tf_op jit(solution)/shard_map/all_to_all | solution.py:99
  83.2 3.6 collective-permute-start
  86.8 0.8 copy-start.3
  87.6 7.5 %copy-start.6 = (f32[8,4,128]{2,1,0:T(4,128)S(1)}, f32[8,4,128]{2,1,0:T(4,128)}, u32[]{:S(2)}) copy-start(f32[8,4,128]{2,1,0:T(4,128)} %param.22) | copy-start | bytes 49156
  104.3 14.9 %copy-start.5 = (f32[32,8,4,128]{3,2,1,0:T(4,128)S(1)}, f32[32,8,4,128]{3,2,1,0:T(4,128)}, u32[]{:S(2)}) copy-start(f32[32,8,4,128]{3,2,1,0:T(4,128)} %param.18) | copy-start | bytes 1572868
  108.9 21.2 %collective-permute-start.2 = (f32[32,6,4,128]{3,0,2,1:T(8,128)}, f32[32,6,4,128]{3,0,2,1:T(8,128)}, u32[]{:S(2)}, u32[]{:S(2)}) collective-permute-start(f32[32,6,4,128]{3,0,2,1:T(8,128)} %copy.92), channel_id=1, source_target_pairs={{0,1},{1,2},{2,3},{3,4},{4,5},{5,6},{6,7},{7,8},{8,9},{9,10},{10,1... | collective-permute-start | bytes 1179656 | tf_op jit(solution)/shard_map/ppermute | solution.py:36
  117.2 14.8 %collective-permute-start.1 = (f32[32,6,4,128]{3,0,2,1:T(8,128)}, f32[32,6,4,128]{3,0,2,1:T(8,128)}, u32[]{:S(2)}, u32[]{:S(2)}) collective-permute-start(f32[32,6,4,128]{3,0,2,1:T(8,128)} %get-tuple-element.40), channel_id=1, source_target_pairs={{0,1},{1,2},{2,3},{3,4},{4,5},{5,6},{6,7},{7,8},{8,9},{9,10},{10,1... | collective-permute-start | bytes 1179656 | tf_op jit(solution)/shard_map/ppermute | solution.py:25
  120.2 16.2 %all-to-all-start.3 = ((f32[32,8,4,128]{3,2,0,1:T(4,128)}), f32[32,8,4,128]{3,2,0,1:T(4,128)}, u32[]{:S(2)}, u32[]{:S(2)}) async-start(f32[32,8,4,128]{3,2,0,1:T(4,128)} %copy.66), calls=%async_computation.3 | async-start | bytes 1048576 | tf_op jit(solution)/shard_map/all_to_all | solution.py:96
  126.1 5.9 %copy-start.7 = (f32[8,4,128]{2,1,0:T(4,128)S(1)}, f32[8,4,128]{2,1,0:T(4,128)}, u32[]{:S(2)}) copy-start(f32[8,4,128]{2,1,0:T(4,128)} %param.20) | copy-start | bytes 49156
  136.4 12.5 %all-to-all-start.2 = ((f32[32,8,4,128]{3,0,2,1:T(8,128)}), f32[32,8,4,128]{3,0,2,1:T(8,128)S(1)}, u32[]{:S(2)}, u32[]{:S(2)}) async-start(f32[32,8,4,128]{3,0,2,1:T(8,128)} %fusion.51), calls=%async_computation.2 | async-start | bytes 1048576 | tf_op jit(solution)/shard_map/all_to_all | solution.py:96
  243.1 11.1 %copy-start.1 = (f32[64,2048]{1,0:T(8,128)}, f32[64,2048]{1,0:T(8,128)S(1)}, u32[]{:S(2)}) copy-start(f32[64,2048]{1,0:T(8,128)S(1)} %fusion.147) | copy-start | bytes 1572868
  255.3 3.6 collective-permute-start.3
  258.9 0.7 copy-start.4
  280.9 16.2 %collective-permute-start.5 = (f32[32,6,4,128]{3,0,2,1:T(8,128)}, f32[32,6,4,128]{3,0,2,1:T(8,128)}, u32[]{:S(2)}, u32[]{:S(2)}) collective-permute-start(f32[32,6,4,128]{3,0,2,1:T(8,128)} %copy.95), channel_id=1, source_target_pairs={{0,1},{1,2},{2,3},{3,4},{4,5},{5,6},{6,7},{7,8},{8,9},{9,10},{10,1... | collective-permute-start | bytes 1179656 | tf_op jit(solution)/shard_map/ppermute | solution.py:36
  289.3 9.7 %collective-permute-start.4 = (f32[32,6,4,128]{3,0,2,1:T(8,128)}, f32[32,6,4,128]{3,0,2,1:T(8,128)}, u32[]{:S(2)}, u32[]{:S(2)}) collective-permute-start(f32[32,6,4,128]{3,0,2,1:T(8,128)} %get-tuple-element.38), channel_id=1, source_target_pairs={{0,1},{1,2},{2,3},{3,4},{4,5},{5,6},{6,7},{7,8},{8,9},{9,10},{10,1... | collective-permute-start | bytes 1179656 | tf_op jit(solution)/shard_map/ppermute | solution.py:25
  297.1 19.1 %copy-start.2 = (f32[64,2048]{1,0:T(8,128)S(1)}, f32[64,2048]{1,0:T(8,128)}, u32[]{:S(2)}) copy-start(f32[64,2048]{1,0:T(8,128)} %copy-done.1) | copy-start | bytes 1572868
  303.5 12.0 %all-to-all-start.5 = ((f32[32,8,4,128]{3,0,2,1:T(8,128)}), f32[32,8,4,128]{3,0,2,1:T(8,128)S(1)}, u32[]{:S(2)}, u32[]{:S(2)}) async-start(f32[32,8,4,128]{3,0,2,1:T(8,128)} %fusion.16), calls=%async_computation.5 | async-start | bytes 1048576 | tf_op jit(solution)/shard_map/all_to_all | solution.py:96
  412.4 11.0 %all-to-all-start.6 = ((f32[64,4,4,128]{3,2,1,0:T(4,128)}), f32[64,4,4,128]{3,2,1,0:T(4,128)S(1)}, u32[]{:S(2)}, u32[]{:S(2)}) async-start(f32[64,4,4,128]{3,2,1,0:T(4,128)} %reshape.195), calls=%async_computation.6 | async-start | bytes 1048576 | tf_op jit(solution)/shard_map/all_to_all | solution.py:99
where the time goes:
time: 426 us; the launch traced here: 424 us
  blocking collectives  209 us (49%)
  other arithmetic  66.8 us (16%)
  local copies, waits for them, and re-layouts  48.4 us (11%)
  starting transfers between devices  46.1 us (11%)
  waiting for transfers between devices  42.7 us (10%)
  matrix products  9.6 us (2%)
    psum x5, blocking collectives, summed(): return lax.psum(matrix, ('band', 'grid'))  198 us
    all_to_all x4, waiting for transfers between devices, to_cells(): lax.all_to_all(block, 'band', split_axis=1, concat_axis=0, tiled=True)  24 us
    another operation x9, other arithmetic, factor_of(): factor = jnp.linalg.cholesky(gram)  19.6 us
    ppermute x2, starting transfers between devices, from_behind(): return lax.ppermute(block, axis, route)  16.7 us
    another operation x6, other arithmetic, factor_of(): inverse = jax.scipy.linalg.solve_triangular(factor, identity, lower=True)  16.6 us
    scatter-add x2, other arithmetic, projector_terms(): jnp.zeros_like(extended).at[:, cell_list]  16 us
    all_to_all x4, starting transfers between devices, to_cells(): lax.all_to_all(block, 'band', split_axis=1, concat_axis=0, tiled=True)  15.7 us
    unnamed x28, local copies, waits for them, and re-layouts  14.7 us
  transfers between devices with their start and end apart: 12, of which 7 were waited for; matrix products, arithmetic and copies ran while one was open for 5% of the time, Pallas kernels for 0%

commit v1 on v0

--- a/solution.py
+++ b/solution.py
@@ -96,7 +96,12 @@
         return lax.all_to_all(block, "band", split_axis=1, concat_axis=0, tiled=True)
 
     def to_states(block):
-        return lax.all_to_all(block, "band", split_axis=0, concat_axis=1, tiled=True)
+        return jnp.concatenate(
+            lax.all_to_all(
+                jnp.stack(jnp.split(block, lax.axis_size("band"), axis=0)), "band", 0, 0
+            ),
+            axis=1,
+        )
 
     def summed(matrix):
         return lax.psum(matrix, ("band", "grid"))

time: 426 us -> 427 us (level)
  no operation moved by 1% of the time
where the time goes in v1:
time: 427 us; the launch traced here: 425 us
  blocking collectives  209 us (49%)
  other arithmetic  68.6 us (16%)
  local copies, waits for them, and re-layouts  47.8 us (11%)
  starting transfers between devices  45.8 us (11%)
  waiting for transfers between devices  42.8 us (10%)
  matrix products  9.61 us (2%)
    psum x5, blocking collectives, summed(): return lax.psum(matrix, ('band', 'grid'))  198 us
    all_to_all x4, waiting for transfers between devices, to_cells(): lax.all_to_all(block, 'band', split_axis=1, concat_axis=0, tiled=True)  24 us
    another operation x9, other arithmetic, factor_of(): factor = jnp.linalg.cholesky(gram)  19.6 us
    another operation x6, other arithmetic, factor_of(): inverse = jax.scipy.linalg.solve_triangular(factor, identity, lower=True)  16.6 us
    ppermute x2, starting transfers between devices, from_behind(): return lax.ppermute(block, axis, route)  16.5 us
    scatter-add x2, other arithmetic, projector_terms(): jnp.zeros_like(extended).at[:, cell_list]  16 us
    all_to_all x4, starting transfers between devices, to_cells(): lax.all_to_all(block, 'band', split_axis=1, concat_axis=0, tiled=True)  15.6 us
    unnamed x28, local copies, waits for them, and re-layouts  15.5 us
  transfers between devices with their start and end apart: 12, of which 7 were waited for; matrix products, arithmetic and copies ran while one was open for 5% of the time, Pallas kernels for 0%

profile of v1, /device:TPU:0, one launch (start us, length us, event | category | flops | bytes accessed | tf_op | source)
XLA Modules:
  0.0 425.2 jit_solution(3593759279724108662)
XLA Ops:
  0.6 1.9 copy.51
  2.6 4.2 all-to-all-start
  7.4 8.1 %all-to-all-done = f32[32,8,4,128]{3,2,0,1:T(4,128)S(1)} async-done(((f32[32,8,4,128]{3,2,0,1:T(4,128)}), f32[32,8,4,128]{3,2,0,1:T(4,128)S(1)}, u32[]{:S(2)}, u32[]{:S(2)}) %all-to-all-start) | async-done | bytes 524320 | tf_op jit(solution)/shard_map/all_to_all | solution.py:96
  16.4 40.0 %psum.35 = f32[64,64]{0,1:T(8,128)S(1)} all-reduce(f32[64,64]{0,1:T(8,128)S(1)} %convolution_multiply_fusion.4), channel_id=1, replica_groups=mesh['band'=2,'grid'=16] {'band','grid'}, use_global_device_ids=true, to_apply=%region_0.0 | all-reduce | flops 4096 | bytes 32768 | tf_op jit(solution)/shard_map/psum | solution.py:107
  56.5 5.8 %cholesky.59 = f32[64,64]{1,0:T(8,128)S(1)} custom-call(f32[64,64]{1,0:T(8,128)S(1)} %fusion.140), custom_call_target="Cholesky" | custom-call | tf_op jit(solution)/shard_map/jit(cholesky)/cholesky | solution.py:72
  63.7 4.9 %custom-call.7 = f32[1,64,64]{1,2,0:T(8,128)S(1)} custom-call(f32[1,64,64]{2,1,0:T(8,128)S(1)} %fusion.134), custom_call_target="InvertDiagBlocksLowerTriangular" | custom-call | tf_op jit(solution)/shard_map/jit(_solve_triangular)/triangular_solve | solution.py:74
  70.0 0.8 pad_maximum_fusion.4
  70.9 3.5 all-to-all-start.1
  74.5 7.9 %all-to-all-done.1 = f32[2,32,4,4,128]{4,1,3,2,0:T(8,128)S(1)} async-done(((f32[2,32,4,4,128]{4,1,3,2,0:T(8,128)}), f32[2,32,4,4,128]{4,1,3,2,0:T(8,128)S(1)}, u32[]{:S(2)}, u32[]{:S(2)}) %all-to-all-start.1) | async-done | bytes 524320 | tf_op jit(solution)/shard_map/all_to_all | solution.py:100
  82.4 0.8 fusion.147
  83.2 1.3 collective-permute-start
  84.5 2.3 collective-permute-done
  86.8 0.8 copy-done.3
  87.7 2.4 copy.57
  90.1 4.8 %gather_fusion = f32[1024,32]{1,0:T(8,128)S(1)} fusion(f32[32,7168]{0,1:T(8,128)} %bitcast.146, s32[1024]{0:T(1024)S(1)} %fusion.141), kind=kCustom, calls=%fused_computation.clone | custom fusion | bytes 266240 | tf_op jit(solution)/shard_map/jit(_take)/gather | solution.py:63
  96.3 8.0 %scatter_custom_fusion = f32[32,7168]{0,1:T(8,128)} fusion(s32[1024]{0:T(1024)S(1)} %bitcast.159, f32[1024,32]{1,0:T(8,128)S(1)} %copy.61, f32[]{:T(128)} %constant.127.clone.1), kind=kCustom, calls=%fused_computation.60 | custom fusion | flops 32768 | bytes 917508 | tf_op jit(solution)/shard_map/scatter-add | solution.py:68
  104.4 3.4 fusion.143
  107.8 1.2 copy.94
  108.9 8.3 %collective-permute-start.2 = (f32[32,6,4,128]{3,0,2,1:T(8,128)}, f32[32,6,4,128]{3,0,2,1:T(8,128)}, u32[]{:S(2)}, u32[]{:S(2)}) collective-permute-start(f32[32,6,4,128]{3,0,2,1:T(8,128)} %copy.94), channel_id=1, source_target_pairs={{0,1},{1,2},{2,3},{3,4},{4,5},{5,6},{6,7},{7,8},{8,9},{9,10},{10,1... | collective-permute-start | bytes 1179656 | tf_op jit(solution)/shard_map/ppermute | solution.py:36
  117.3 2.0 collective-permute-start.1
  119.3 0.9 copy.67
  120.2 4.2 all-to-all-start.3
  124.4 1.7 slice.416
  126.2 2.6 copy.93
  128.8 1.4 copy.92
  130.1 1.9 add_dynamic-update-slice_fusion.1
  132.1 4.3 %fusion.51 = f32[32,8,4,128]{3,0,2,1:T(8,128)} fusion(f32[32,8,4,128]{3,0,2,1:T(8,128)} %add_dynamic-update-slice_fusion.1, f32[32,8,4,128]{3,0,2,1:T(8,128)S(1)} %bitcast.141, f32[32,6,4,128]{3,0,2,1:T(8,128)} %collective-permute-done.1, f32[32,6,4,128]{3,0,2,1:T(8,128)} %copy-done.3, f32[8,4,128]{2,1,0:T(4,128)S(1)} %copy-done.7), kind=kLoop, calls=%fused_computation.150 | loop fusion | flops 8388608 | bytes 2375680 | tf_op jit(solution)/shard_map/add | solution.py:127
  136.4 3.7 all-to-all-start.2
  140.1 1.1 copy.104
  141.5 7.5 %all-to-all-done.2 = f32[32,8,4,128]{3,0,2,1:T(8,128)S(1)} async-done(((f32[32,8,4,128]{3,0,2,1:T(8,128)}), f32[32,8,4,128]{3,0,2,1:T(8,128)S(1)}, u32[]{:S(2)}, u32[]{:S(2)}) %all-to-all-start.2) | async-done | bytes 524320 | tf_op jit(solution)/shard_map/all_to_all | solution.py:96
  150.1 39.0 %psum.36 = f32[64,64]{0,1:T(8,128)S(1)} all-reduce(f32[64,64]{0,1:T(8,128)S(1)} %convolution_multiply_fusion.3), channel_id=1, replica_groups=mesh['band'=2,'grid'=16] {'band','grid'}, use_global_device_ids=true, to_apply=%region_4.8 | all-reduce | flops 4096 | bytes 32768 | tf_op jit(solution)/shard_map/psum | solution.py:107
  190.8 39.3 %psum.37 = f32[64,64]{0,1:T(8,128)S(1)} all-reduce(f32[64,64]{0,1:T(8,128)S(1)} %convolution_multiply_fusion.2), channel_id=1, replica_groups=mesh['band'=2,'grid'=16] {'band','grid'}, use_global_device_ids=true, to_apply=%region_5.9 | all-reduce | flops 4096 | bytes 32768 | tf_op jit(solution)/shard_map/psum | solution.py:107
  230.2 5.8 %cholesky.70 = f32[64,64]{1,0:T(8,128)S(1)} custom-call(f32[64,64]{1,0:T(8,128)S(1)} %fusion.138), custom_call_target="Cholesky" | custom-call | tf_op jit(solution)/shard_map/jit(cholesky)/cholesky | solution.py:72
  236.8 0.7 select_bitcast_fusion.1
  237.4 4.9 %custom-call.8 = f32[1,64,64]{1,2,0:T(8,128)S(1)} custom-call(f32[1,64,64]{2,1,0:T(8,128)S(1)} %get-tuple-element.32), custom_call_target="InvertDiagBlocksLowerTriangular" | custom-call | tf_op jit(solution)/shard_map/jit(_solve_triangular)/triangular_solve | solution.py:74
  243.2 0.8 copy-done.1
  244.6 10.8 %all_to_all.75 = f32[2,32,4,4,128]{4,1,3,2,0:T(8,128)S(1)} all-to-all(f32[2,32,4,4,128]{4,1,3,2,0:T(8,128)S(1)} %pad_maximum_fusion.5), channel_id=1, replica_groups=mesh['band'=2,'grid'=16] {'band'}, dimensions={0} | all-to-all | bytes 1048576 | tf_op jit(solution)/shard_map/all_to_all | solution.py:100
  255.4 0.8 fusion.145
  256.2 1.3 collective-permute-start.3
  257.5 2.3 collective-permute-done.3
  259.8 0.7 copy-done.4
  260.6 2.4 copy.73
  263.1 4.8 %gather_fusion.1 = f32[1024,32]{1,0:T(8,128)S(1)} fusion(f32[32,7168]{0,1:T(8,128)} %bitcast.145, s32[1024]{0:T(1024)S(1)} %fusion.141), kind=kCustom, calls=%fused_computation.1.clone | custom fusion | bytes 266240 | tf_op jit(solution)/shard_map/jit(_take)/gather | solution.py:63
  269.3 8.0 %scatter_custom_fusion.1 = f32[32,7168]{0,1:T(8,128)} fusion(s32[1024]{0:T(1024)S(1)} %bitcast.160, f32[1024,32]{1,0:T(8,128)S(1)} %copy.76, f32[]{:T(128)} %constant.127.clone.1), kind=kCustom, calls=%fused_computation.58 | custom fusion | flops 32768 | bytes 917508 | tf_op jit(solution)/shard_map/scatter-add | solution.py:68
  277.3 3.3 fusion.142
  280.7 1.2 copy.97
  281.9 8.2 %collective-permute-start.5 = (f32[32,6,4,128]{3,0,2,1:T(8,128)}, f32[32,6,4,128]{3,0,2,1:T(8,128)}, u32[]{:S(2)}, u32[]{:S(2)}) collective-permute-start(f32[32,6,4,128]{3,0,2,1:T(8,128)} %copy.97), channel_id=1, source_target_pairs={{0,1},{1,2},{2,3},{3,4},{4,5},{5,6},{6,7},{7,8},{8,9},{9,10},{10,1... | collective-permute-start | bytes 1179656 | tf_op jit(solution)/shard_map/ppermute | solution.py:36
  290.0 2.0 collective-permute-start.4
  292.1 1.7 slice.443
  293.8 2.6 copy.96
  296.4 1.4 copy.95
  297.8 2.0 add_dynamic-update-slice_fusion
  299.8 4.5 %fusion.16 = f32[32,8,4,128]{3,0,2,1:T(8,128)} fusion(f32[32,8,4,128]{3,0,2,1:T(8,128)} %add_dynamic-update-slice_fusion, f32[32,8,4,128]{3,0,2,1:T(8,128)S(1)} %bitcast.144, f32[32,6,4,128]{3,0,2,1:T(8,128)} %collective-permute-done.4, f32[32,6,4,128]{3,0,2,1:T(8,128)} %copy-done.4, f32[8,4,128]{2,1,0:T(4,128)S(1)} %copy-done.7), kind=kLoop, calls=%fused_computation.115 | loop fusion | flops 8388608 | bytes 2375680 | tf_op jit(solution)/shard_map/add | solution.py:127
  304.3 3.5 all-to-all-start.5
  307.8 8.5 %all-to-all-done.5 = f32[32,8,4,128]{3,0,2,1:T(8,128)S(1)} async-done(((f32[32,8,4,128]{3,0,2,1:T(8,128)}), f32[32,8,4,128]{3,0,2,1:T(8,128)S(1)}, u32[]{:S(2)}, u32[]{:S(2)}) %all-to-all-start.5) | async-done | bytes 524320 | tf_op jit(solution)/shard_map/all_to_all | solution.py:96
  317.4 39.3 %psum.38 = f32[64,64]{0,1:T(8,128)S(1)} all-reduce(f32[64,64]{0,1:T(8,128)S(1)} %convolution_multiply_fusion.1), channel_id=1, replica_groups=mesh['band'=2,'grid'=16] {'band','grid'}, use_global_device_ids=true, to_apply=%region_7.11 | all-reduce | flops 4096 | bytes 32768 | tf_op jit(solution)/shard_map/psum | solution.py:107
  358.6 40.4 %psum.39 = f32[64,64]{0,1:T(8,128)S(1)} all-reduce(f32[64,64]{0,1:T(8,128)S(1)} %convolution_multiply_fusion), channel_id=1, replica_groups=mesh['band'=2,'grid'=16] {'band','grid'}, use_global_device_ids=true, to_apply=%region_8.12 | all-reduce | flops 4096 | bytes 32768 | tf_op jit(solution)/shard_map/psum | solution.py:107
  399.1 5.8 %cholesky.81 = f32[64,64]{1,0:T(8,128)S(1)} custom-call(f32[64,64]{1,0:T(8,128)S(1)} %fusion.136), custom_call_target="Cholesky" | custom-call | tf_op jit(solution)/shard_map/jit(cholesky)/cholesky | solution.py:72
  405.6 0.7 select_bitcast_fusion
  406.3 4.9 %custom-call.9 = f32[1,64,64]{1,2,0:T(8,128)S(1)} custom-call(f32[1,64,64]{2,1,0:T(8,128)S(1)} %get-tuple-element.30), custom_call_target="InvertDiagBlocksLowerTriangular" | custom-call | tf_op jit(solution)/shard_map/jit(_solve_triangular)/triangular_solve | solution.py:74
  412.4 0.9 pad_maximum_fusion.6
  413.3 3.5 all-to-all-start.6
  418.1 6.2 %all-to-all-done.6 = f32[2,32,4,4,128]{4,3,2,1,0:T(4,128)S(1)} async-done(((f32[2,32,4,4,128]{4,3,2,1,0:T(4,128)}), f32[2,32,4,4,128]{4,3,2,1,0:T(4,128)S(1)}, u32[]{:S(2)}, u32[]{:S(2)}) %all-to-all-start.6) | async-done | bytes 524320 | tf_op jit(solution)/shard_map/all_to_all | solution.py:100
  424.3 0.9 copy.84
  (95 shorter events, 18.1 us)
Async XLA Ops:
  0.6 189.0 %copy-start = (f32[64,64]{1,0:T(8,128)S(1)}, f32[64,64]{1,0:T(8,128)}, u32[]{:S(2)}) copy-start(f32[64,64]{1,0:T(8,128)} %param.19) | copy-start | bytes 49156
  2.6 12.9 %all-to-all-start = ((f32[32,8,4,128]{3,2,0,1:T(4,128)}), f32[32,8,4,128]{3,2,0,1:T(4,128)S(1)}, u32[]{:S(2)}, u32[]{:S(2)}) async-start(f32[32,8,4,128]{3,2,0,1:T(4,128)} %copy.51), calls=%async_computation | async-start | bytes 1048576 | tf_op jit(solution)/shard_map/all_to_all | solution.py:96
  15.8 58.6 %copy-start.9 = (f32[8,4]{0,1:T(4,128)S(1)}, f32[8,4]{0,1:T(4,128)}, u32[]{:S(2)}) copy-start(f32[8,4]{0,1:T(4,128)} %param.23) | copy-start | bytes 388
  15.8 58.6 %copy-start.8 = (s32[8,128]{1,0:T(8,128)S(1)}, s32[8,128]{1,0:T(8,128)}, u32[]{:S(2)}) copy-start(s32[8,128]{1,0:T(8,128)} %param.21) | copy-start | bytes 12292
  70.9 11.5 %all-to-all-start.1 = ((f32[2,32,4,4,128]{4,1,3,2,0:T(8,128)}), f32[2,32,4,4,128]{4,1,3,2,0:T(8,128)S(1)}, u32[]{:S(2)}, u32[]{:S(2)}) async-start(f32[2,32,4,4,128]{4,1,3,2,0:T(8,128)} %pad_maximum_fusion.4), calls=%async_computation.1 | async-start | bytes 1048576 | tf_op jit(solution)/shard_map/all_to_all | solution.py:100
  83.2 3.6 collective-permute-start
  86.8 0.8 copy-start.3
  87.6 7.5 %copy-start.6 = (f32[8,4,128]{2,1,0:T(4,128)S(1)}, f32[8,4,128]{2,1,0:T(4,128)}, u32[]{:S(2)}) copy-start(f32[8,4,128]{2,1,0:T(4,128)} %param.22) | copy-start | bytes 49156
  104.4 14.9 %copy-start.5 = (f32[32,8,4,128]{3,2,1,0:T(4,128)S(1)}, f32[32,8,4,128]{3,2,1,0:T(4,128)}, u32[]{:S(2)}) copy-start(f32[32,8,4,128]{3,2,1,0:T(4,128)} %param.18) | copy-start | bytes 1572868
  108.9 21.2 %collective-permute-start.2 = (f32[32,6,4,128]{3,0,2,1:T(8,128)}, f32[32,6,4,128]{3,0,2,1:T(8,128)}, u32[]{:S(2)}, u32[]{:S(2)}) collective-permute-start(f32[32,6,4,128]{3,0,2,1:T(8,128)} %copy.94), channel_id=1, source_target_pairs={{0,1},{1,2},{2,3},{3,4},{4,5},{5,6},{6,7},{7,8},{8,9},{9,10},{10,1... | collective-permute-start | bytes 1179656 | tf_op jit(solution)/shard_map/ppermute | solution.py:36
  117.3 14.8 %collective-permute-start.1 = (f32[32,6,4,128]{3,0,2,1:T(8,128)}, f32[32,6,4,128]{3,0,2,1:T(8,128)}, u32[]{:S(2)}, u32[]{:S(2)}) collective-permute-start(f32[32,6,4,128]{3,0,2,1:T(8,128)} %get-tuple-element.44), channel_id=1, source_target_pairs={{0,1},{1,2},{2,3},{3,4},{4,5},{5,6},{6,7},{7,8},{8,9},{9,10},{10,1... | collective-permute-start | bytes 1179656 | tf_op jit(solution)/shard_map/ppermute | solution.py:25
  120.2 16.2 %all-to-all-start.3 = ((f32[32,8,4,128]{3,2,0,1:T(4,128)}), f32[32,8,4,128]{3,2,0,1:T(4,128)}, u32[]{:S(2)}, u32[]{:S(2)}) async-start(f32[32,8,4,128]{3,2,0,1:T(4,128)} %copy.67), calls=%async_computation.3 | async-start | bytes 1048576 | tf_op jit(solution)/shard_map/all_to_all | solution.py:96
  126.2 5.9 %copy-start.7 = (f32[8,4,128]{2,1,0:T(4,128)S(1)}, f32[8,4,128]{2,1,0:T(4,128)}, u32[]{:S(2)}) copy-start(f32[8,4,128]{2,1,0:T(4,128)} %param.20) | copy-start | bytes 49156
  136.4 12.5 %all-to-all-start.2 = ((f32[32,8,4,128]{3,0,2,1:T(8,128)}), f32[32,8,4,128]{3,0,2,1:T(8,128)S(1)}, u32[]{:S(2)}, u32[]{:S(2)}) async-start(f32[32,8,4,128]{3,0,2,1:T(8,128)} %fusion.51), calls=%async_computation.2 | async-start | bytes 1048576 | tf_op jit(solution)/shard_map/all_to_all | solution.py:96
  243.2 0.8 copy-start.1
  256.2 3.6 collective-permute-start.3
  259.8 0.7 copy-start.4
  281.9 15.9 %collective-permute-start.5 = (f32[32,6,4,128]{3,0,2,1:T(8,128)}, f32[32,6,4,128]{3,0,2,1:T(8,128)}, u32[]{:S(2)}, u32[]{:S(2)}) collective-permute-start(f32[32,6,4,128]{3,0,2,1:T(8,128)} %copy.97), channel_id=1, source_target_pairs={{0,1},{1,2},{2,3},{3,4},{4,5},{5,6},{6,7},{7,8},{8,9},{9,10},{10,1... | collective-permute-start | bytes 1179656 | tf_op jit(solution)/shard_map/ppermute | solution.py:36
  290.0 9.7 %collective-permute-start.4 = (f32[32,6,4,128]{3,0,2,1:T(8,128)}, f32[32,6,4,128]{3,0,2,1:T(8,128)}, u32[]{:S(2)}, u32[]{:S(2)}) collective-permute-start(f32[32,6,4,128]{3,0,2,1:T(8,128)} %get-tuple-element.40), channel_id=1, source_target_pairs={{0,1},{1,2},{2,3},{3,4},{4,5},{5,6},{6,7},{7,8},{8,9},{9,10},{10,1... | collective-permute-start | bytes 1179656 | tf_op jit(solution)/shard_map/ppermute | solution.py:25
  297.8 19.1 %copy-start.2 = (f32[64,2048]{1,0:T(8,128)S(1)}, f32[64,2048]{1,0:T(8,128)}, u32[]{:S(2)}) copy-start(f32[64,2048]{1,0:T(8,128)} %copy-done.1) | copy-start | bytes 1572868
  304.3 12.0 %all-to-all-start.5 = ((f32[32,8,4,128]{3,0,2,1:T(8,128)}), f32[32,8,4,128]{3,0,2,1:T(8,128)S(1)}, u32[]{:S(2)}, u32[]{:S(2)}) async-start(f32[32,8,4,128]{3,0,2,1:T(8,128)} %fusion.16), calls=%async_computation.5 | async-start | bytes 1048576 | tf_op jit(solution)/shard_map/all_to_all | solution.py:96
  413.3 11.0 %all-to-all-start.6 = ((f32[2,32,4,4,128]{4,3,2,1,0:T(4,128)}), f32[2,32,4,4,128]{4,3,2,1,0:T(4,128)S(1)}, u32[]{:S(2)}, u32[]{:S(2)}) async-start(f32[2,32,4,4,128]{4,3,2,1,0:T(4,128)} %pad_maximum_fusion.6), calls=%async_computation.6 | async-start | bytes 1048576 | tf_op jit(solution)/shard_map/all_to_all | solution.py:100
